TPU v7x, 32 devices: a whole 2x2x4 slice. The times are simulated.
32 devices in a mesh: dp: 8 (over y, x, core), chan: 4 (over z).
Axes of the slice: x: 2, y: 2, z: 4, core: 2. Of those that a mesh axis runs over, the one named last changes fastest.
Arguments:
- inputs: bfloat16 [192, 152, 800], P('dp', None, 'chan'), may hold values from -6 to 6
- ocean_mask: int32 [192, 152], P('dp'), may hold values 0 or 1
- counts: int32 [4], replicated, may hold values from 1 to 2
- kernel: float32 [7, 7, 800], P(None, None, 'chan'), may hold values from -0.875 to 0.875
- conv_bias: float32 [800], P('chan'), may hold values from -3 to 3
- norm_gain: float32 [800], P('chan'), may hold values from 0.5 to 1.5
- norm_bias: float32 [800], P('chan'), may hold values from -3 to 3
- weight_in: bfloat16 [800, 3200], P(None, 'chan'), may hold values from -0.21875 to 0.21875
- bias_in: float32 [3200], P('chan'), may hold values from -3 to 3
- weight_out: bfloat16 [3200, 800], P('chan'), may hold values from -0.21875 to 0.21875
- bias_out: float32 [800], P('chan'), may hold values from -3 to 3
- cotangent: bfloat16 [192, 152, 800], P('dp', None, 'chan'), may hold values from -6 to 6
Outputs:
- output: bfloat16 [192, 152, 800], P('dp', None, 'chan')
- grad_inputs: float32 [192, 152, 800], P('dp', None, 'chan')
- grad_kernel: float32 [7, 7, 800], P(None, None, 'chan')
- grad_conv_bias: float32 [800], P('chan')
- grad_gain: float32 [800], P('chan')
- grad_norm_bias: float32 [800], P('chan')
- grad_weight_in: float32 [800, 3200], P(None, 'chan')
- grad_bias_in: float32 [3200], P('chan')
- grad_weight_out: float32 [3200, 800], P('chan')
- grad_bias_out: float32 [800], P('chan')
All inputs are finite; a program needn't handle non-finite values. No bound on the sum of `ocean_mask` on one device may be relied on, other than what follows from the above.
Results may differ from a plain program's by a relative error of at most 0.0057.
Values may be sent and summed in bfloat16 or wider, within the bound.
No kernel may reach another device: no remote copies, remote signals or barrier semaphores. Data moves between devices by JAX's collectives and lax.ppermute only.
A program may use at most 192 MiB of HBM per device.

v0:
```python
import jax
import jax.numpy as jnp
from jax import lax
from jax.sharding import PartitionSpec as P

CH = 800
GROUPS = 8
HISTORY = 2
SPAN = 2
EPSILON = 1e-05


def swapped(block, axis, distance):
    count = lax.axis_size(axis)
    route = []
    for low in range(count):
        high = low | 1 << distance
        if high != low and high < count:
            route += [(low, high), (high, low)]
    return lax.ppermute(block, axis, route)


def with_rim(values, rim, top_valid, bottom_valid):
    return jnp.concatenate([rim * top_valid, values, rim * bottom_valid], axis=0)


def local_groups(values, group_size):
    height, across, local_ch = values.shape
    return jnp.sum(
        values.reshape(height, across, local_ch // group_size, group_size), axis=(0, 1, 3)
    )


def spread_groups(summed, group_size, members):
    return jnp.repeat(summed, group_size) / members


def gelu_slope(hidden):
    cumulative = 0.5 * (1.0 + lax.erf(hidden * 0.7071067811865476))
    density = jnp.exp(-0.5 * hidden * hidden) * 0.3989422804014327
    return cumulative + hidden * density


def body(
    inputs,
    ocean_mask,
    counts,
    kernel,
    conv_bias,
    norm_gain,
    norm_bias,
    weight_in,
    bias_in,
    weight_out,
    bias_out,
    cotangent,
):
    height, across, local_ch = inputs.shape
    pixels = height * across
    group_size = CH // GROUPS
    members = height * SPAN * across * group_size
    dp_index = lax.axis_index("dp")
    sample = dp_index // SPAN
    within = dp_index % SPAN
    sample_ids = jnp.arange(counts.shape[0])
    count_here = jnp.sum(jnp.where(sample_ids == sample, counts, 0))
    channel = lax.axis_index("chan") * local_ch + jnp.arange(local_ch)
    history_keep = (channel // (CH // HISTORY) < count_here).astype(jnp.float32)
    wet_cells = ocean_mask.astype(jnp.float32)[:, :, None]
    masked = inputs.astype(jnp.float32) * wet_cells * history_keep
    top_valid = (within > 0).astype(jnp.float32)
    bottom_valid = (within == 0).astype(jnp.float32)
    is_upper = within == 0
    masked_low = masked.astype(jnp.bfloat16)
    outgoing = jnp.where(is_upper, masked_low[height - 3 :], masked_low[:3])
    rim_in = swapped(outgoing, "dp", 0).astype(jnp.float32)
    padded = jnp.pad(with_rim(masked, rim_in, top_valid, bottom_valid), ((0, 0), (3, 3), (0, 0)))
    convolved = jnp.zeros((height, across, local_ch), jnp.float32) + conv_bias
    for row_shift in range(7):
        for col_shift in range(7):
            convolved = (
                convolved
                + padded[row_shift : row_shift + height, col_shift : col_shift + across]
                * kernel[row_shift, col_shift]
            )
    own_sum = local_groups(convolved, group_size)
    centre = spread_groups(own_sum + swapped(own_sum, "dp", 0), group_size, members)
    offset = convolved - centre
    own_sq = local_groups(offset * offset, group_size)
    spread = spread_groups(own_sq + swapped(own_sq, "dp", 0), group_size, members)
    inverse = lax.rsqrt(spread + EPSILON)
    standard = offset * inverse
    normed = (standard * norm_gain + norm_bias).astype(jnp.bfloat16).reshape(pixels, local_ch)
    grad_res = cotangent.astype(jnp.float32) * wet_cells
    grad_branch = grad_res.reshape(pixels, local_ch).astype(jnp.bfloat16)
    grad_bias_out = jnp.sum(grad_branch.astype(jnp.float32), 0)
    gathered = lax.all_gather(normed, "chan", axis=1, tiled=True)
    hidden = jnp.dot(gathered, weight_in, preferred_element_type=jnp.float32) + bias_in
    active = jax.nn.gelu(hidden, approximate=False).astype(jnp.bfloat16)
    partial_value = jnp.dot(active, weight_out, preferred_element_type=jnp.float32)
    branch = lax.psum_scatter(partial_value, "chan", scatter_dimension=1, tiled=True) + bias_out
    output = (wet_cells * (masked + branch.reshape(height, across, local_ch))).astype(jnp.bfloat16)
    grad_gathered = lax.all_gather(grad_branch, "chan", axis=1, tiled=True)
    grad_active = lax.dot_general(
        grad_gathered, weight_out, (((1,), (1,)), ((), ())), preferred_element_type=jnp.float32
    )
    grad_weight_out = lax.dot_general(
        active, grad_gathered, (((0,), (0,)), ((), ())), preferred_element_type=jnp.float32
    )
    grad_hidden = (grad_active * gelu_slope(hidden)).astype(jnp.bfloat16)
    grad_bias_in = jnp.sum(grad_hidden.astype(jnp.float32), 0)
    grad_weight_in = lax.dot_general(
        gathered, grad_hidden, (((0,), (0,)), ((), ())), preferred_element_type=jnp.float32
    )
    grad_part = lax.dot_general(
        grad_hidden, weight_in, (((1,), (1,)), ((), ())), preferred_element_type=jnp.float32
    )
    grad_normed = lax.psum_scatter(grad_part, "chan", scatter_dimension=1, tiled=True).reshape(
        height, across, local_ch
    )
    grad_gain = jnp.sum(grad_normed * standard, (0, 1))
    grad_norm_bias = jnp.sum(grad_normed, (0, 1))
    grad_standard = grad_normed * norm_gain
    own_pair = jnp.stack(
        [
            local_groups(grad_standard, group_size),
            local_groups(grad_standard * standard, group_size),
        ]
    )
    both_pair = own_pair + swapped(own_pair, "dp", 0)
    mean_first = spread_groups(both_pair[0], group_size, members)
    mean_second = spread_groups(both_pair[1], group_size, members)
    grad_conv = inverse * (grad_standard - mean_first - standard * mean_second)
    grad_conv_bias = jnp.sum(grad_conv, (0, 1))
    kernel_rows = []
    for row_shift in range(7):
        for col_shift in range(7):
            kernel_rows.append(
                jnp.sum(
                    grad_conv
                    * padded[row_shift : row_shift + height, col_shift : col_shift + across],
                    (0, 1),
                )
            )
    grad_kernel = jnp.stack(kernel_rows).reshape(7, 7, local_ch)
    grad_out_rows = jnp.where(is_upper, grad_conv[height - 3 :], grad_conv[:3])
    grad_rim = swapped(grad_out_rows.astype(jnp.bfloat16), "dp", 0).astype(grad_out_rows.dtype)
    grad_padded = jnp.pad(
        with_rim(grad_conv, grad_rim, top_valid, bottom_valid), ((0, 0), (3, 3), (0, 0))
    )
    grad_masked = jnp.zeros((height, across, local_ch), jnp.float32)
    for row_shift in range(7):
        for col_shift in range(7):
            grad_masked = (
                grad_masked
                + grad_padded[
                    6 - row_shift : 6 - row_shift + height, 6 - col_shift : 6 - col_shift + across
                ]
                * kernel[row_shift, col_shift]
            )
    grad_inputs = wet_cells * history_keep * (grad_res + grad_masked)
    (
        grad_kernel,
        grad_conv_bias,
        grad_gain,
        grad_norm_bias,
        grad_weight_in,
        grad_bias_in,
        grad_weight_out,
        grad_bias_out,
    ) = lax.psum(
        (
            grad_kernel,
            grad_conv_bias,
            grad_gain,
            grad_norm_bias,
            grad_weight_in,
            grad_bias_in,
            grad_weight_out,
            grad_bias_out,
        ),
        "dp",
    )
    return (
        output,
        grad_inputs,
        grad_kernel,
        grad_conv_bias,
        grad_gain,
        grad_norm_bias,
        grad_weight_in,
        grad_bias_in,
        grad_weight_out,
        grad_bias_out,
    )


def solution(mesh):
    in_specs = (
        P("dp", None, "chan"),
        P("dp", None),
        P(),
        P(None, None, "chan"),
        P("chan"),
        P("chan"),
        P("chan"),
        P(None, "chan"),
        P("chan"),
        P("chan", None),
        P("chan"),
        P("dp", None, "chan"),
    )
    out_specs = (
        P("dp", None, "chan"),
        P("dp", None, "chan"),
        P(None, None, "chan"),
        P("chan"),
        P("chan"),
        P("chan"),
        P(None, "chan"),
        P("chan"),
        P("chan", None),
        P("chan"),
    )
    return jax.shard_map(body, mesh=mesh, in_specs=in_specs, out_specs=out_specs, check_vma=False)
```

profile of v0, /device:TPU:0, one launch (start us, length us, event | category | flops | bytes accessed | tf_op | source)
XLA Modules:
  0.0 971.4 jit_solution(3660102376321455770)
XLA Ops:
  7.3 0.8 convert_element_type.63
  8.1 1.3 fusion.84
  9.4 0.7 compare_convert_fusion
  10.1 5.1 convert_reduce_fusion.1
  15.2 0.5 collective-permute-start
  15.9 0.5 fusion.90
  16.6 0.6 fusion.91
  17.2 0.1 convert_multiply_fusion.4
  17.4 4.5 select_maximum_fusion.2
  22.3 75.7 %fusion.88 = (f32[200]{0:T(256)S(1)}, f32[24,152,200]{2,1,0:T(8,128)}) fusion(f32[200]{0:T(256)} %bitcast.48, f32[30,158,200]{2,1,0:T(8,128)} %select_maximum_fusion.2, f32[200]{0:T(256)} %bitcast.47, f32[200]{0:T(256)S(1)} %bitcast.130, f32[200]{0:T(256)S(1)} %bitcast.132, f32[3,152,200]{2,1,0:T(8,128)S(1)} %get-tuple-element.86, ...), kind=kLoop, calls=%fused_computation.242 | loop fusion | flops 76607800 | bytes 129180000 | tf_op jit(solution)/shard_map/reduce_sum | solution.py:29
  98.0 0.1 reduce_sum.561
  98.1 0.1 reduce_sum.562
  98.2 0.1 collective-permute-start.1
  98.3 1.1 collective-permute-done.1
  99.4 0.1 broadcast_in_dim.13
  99.5 0.1 div.45
  99.5 2.6 multiply_reduce_fusion.51
  102.1 0.1 reduce_sum.564
  102.2 0.1 reduce_sum.565
  102.3 0.3 collective-permute-start.2
  102.6 0.9 collective-permute-done.2
  103.5 0.1 broadcast_in_dim.14
  103.6 0.1 rsqrt.12
  103.7 2.7 add_convert_fusion
  106.4 2.5 copy.31
  108.9 3.8 copy.33
  112.7 0.2 reduce-scatter.9.cloned.1.call-start
  112.9 108.1 %all-gather.3.cloned.1.call-done = bf16[3648,800]{0,1:T(8,128)(2,1)} async-done(((bf16[3648,200]{0,1:T(8,128)(2,1)}), bf16[3648,800]{0,1:T(8,128)(2,1)}) %all-gather.3.cloned.1.call-update) | async-done | bytes 5836816 | tf_op jit(solution)/shard_map/all_gather | solution.py:97
  221.0 35.8 %fusion.2 = (bf16[3648,800]{0,1:T(8,128)(2,1)}, f32[3648,800]{0,1:T(8,128)}) fusion(f32[800]{0:T(1024)S(1)} %copy-done.101, bf16[3648,800]{0,1:T(8,128)(2,1)} %all-gather.3.cloned.1.call-done, bf16[800,800]{1,0:T(8,128)(2,1)S(1)} %copy-done), kind=kOutput, calls=%fused_computation.4 | convolution fusion | flops 4862054400 | bytes 24630400 | tf_op jit(solution)/shard_map/dot_general | solution.py:98
  256.8 74.2 %all-gather.5.cloned.1.call-done = bf16[3648,800]{0,1:T(8,128)(2,1)} async-done(((bf16[3648,200]{0,1:T(8,128)(2,1)}), bf16[3648,800]{0,1:T(8,128)(2,1)}) %all-gather.5.cloned.1.call-update) | async-done | bytes 5836816 | tf_op jit(solution)/shard_map/all_gather | solution.py:103
  331.0 12.0 %convert_reduce_fusion = (f32[800]{0:T(1024)S(1)}, bf16[3648,800]{0,1:T(8,128)(2,1)S(1)}) fusion(f32[3648,800]{0,1:T(8,128)} %get-tuple-element.141, f32[800]{0:T(1024)S(1)} %copy-done.101, bf16[800,800]{1,0:T(8,128)(2,1)} %param.21, bf16[3648,800]{0,1:T(8,128)(2,1)} %all-gather.5.cloned.1.call-done), kind=kOutput, calls=%fused_computation.11 | convolution fusion | flops 4707378176 | bytes 24633600 | tf_op jit(solution)/shard_map/dot_general | solution.py:104
  343.1 2.6 copy-done.102
  345.6 9.2 fusion.95
  354.9 0.3 reduce-scatter.7.cloned.1.call-start
  355.2 1.1 copy-done.100
  356.2 11.5 %fusion.92 = f32[3648,800]{0,1:T(8,128)} fusion(bf16[3648,800]{0,1:T(8,128)(2,1)} %get-tuple-element.140, bf16[800,800]{1,0:T(8,128)(2,1)S(1)} %copy-done.100), kind=kOutput, calls=%fused_computation.246 | convolution fusion | flops 4669440000 | bytes 18790400 | tf_op jit(solution)/shard_map/dot_general | solution.py:100
  367.8 11.4 %fusion.94 = f32[800,800]{1,0:T(8,128)} fusion(bf16[3648,800]{0,1:T(8,128)(2,1)} %get-tuple-element.140, bf16[3648,800]{0,1:T(8,128)(2,1)} %all-gather.5.cloned.1.call-done), kind=kOutput, calls=%fused_computation.248 | convolution fusion | flops 4669440000 | bytes 14233600 | tf_op jit(solution)/shard_map/dot_general | solution.py:107
  379.2 11.5 %fusion.93 = f32[800,800]{1,0:T(8,128)} fusion(bf16[3648,800]{0,1:T(8,128)(2,1)} %all-gather.3.cloned.1.call-done, bf16[3648,800]{0,1:T(8,128)(2,1)} %copy-done.102), kind=kOutput, calls=%fused_computation.247 | convolution fusion | flops 4669440000 | bytes 14233600 | tf_op jit(solution)/shard_map/dot_general | solution.py:112
  390.7 164.1 %reduce-scatter.9.cloned.1.call-done = f32[3648,200]{0,1:T(8,128)} async-done(((f32[3648,800]{0,1:T(8,128)}), f32[3648,200]{0,1:T(8,128)}) %reduce-scatter.9.cloned.1.call-update) | async-done | bytes 2918416
  554.8 2.3 fusion.86
  557.1 0.1 reduce_sum.567
  557.2 0.1 reduce_sum.568
  557.3 4.9 copy.34
  562.2 5.3 multiply_reduce_fusion
  567.5 0.1 reduce_sum.570
  567.6 0.1 reduce_sum.571
  567.7 0.1 collective-permute-start.3
  567.8 191.2 %reduce-scatter.7.cloned.1.call-done = f32[3648,200]{0,1:T(8,128)} async-done(((f32[3648,800]{0,1:T(8,128)}), f32[3648,200]{0,1:T(8,128)}) %reduce-scatter.7.cloned.1.call-update) | async-done | bytes 2918416
  759.0 4.9 copy.32
  763.9 4.1 broadcast_add_fusion
  768.1 0.1 broadcast_in_dim.15
  768.1 0.1 div.49
  768.2 0.1 broadcast_in_dim.16
  768.3 0.1 div.52
  768.4 38.1 %multiply_reduce_fusion.1 = (f32[200]{0:T(256)S(1)}, f32[200]{0:T(256)S(1)}, f32[200]{0:T(256)S(1)}, f32[200]{0:T(256)S(1)}, f32[200]{0:T(256)S(1)}, /*index=5*/...) fusion(f32[30,158,200]{2,1,0:T(8,128)} %select_maximum_fusion.2, ...), kind=kLoop, calls=%fused_computation.162 | loop fusion | flops 31369200 | bytes 61304800 | tf_op jit(solution)/shard_map/reduce_sum | solution.py:139
  806.6 30.1 %multiply_reduce_fusion.2 = (f32[200]{0:T(256)S(1)}, f32[200]{0:T(256)S(1)}, f32[200]{0:T(256)S(1)}, f32[200]{0:T(256)S(1)}, f32[200]{0:T(256)S(1)}, /*index=5*/...) fusion(f32[24,152,200]{2,1,0:T(8,128)} %get-tuple-element.77, ...), kind=kLoop, calls=%fused_computation.163 | loop fusion | flops 26262000 | bytes 55464000 | tf_op jit(solution)/shard_map/reduce_sum | solution.py:139
  836.8 8.8 multiply_reduce_fusion.4
  845.6 3.4 multiply_reduce_fusion.43
  849.1 0.2 stack.211
  849.2 26.3 %all-reduce.4 = (f32[7,7,200]{2,1,0:T(8,128)}, f32[200]{0:T(256)}, f32[200]{0:T(256)}, f32[200]{0:T(256)}, f32[800]{0:T(1024)}, /*index=5*/f32[200]{0:T(256)}) all-reduce(f32[7,7,200]{2,1,0:T(8,128)S(1)} %reshape.110, f32[200]{0:T(256)S(1)} %get-tuple-element.63, ...), channel_id=1, replica_groups=mesh['dp'=8,'chan'=4] {'dp'}, use_global_device_ids=true, to_apply=%region_60.61 | all-reduce | flops 11400 | bytes 91200 | tf_op jit(solution)/shard_map/psum | solution.py:171
  876.0 4.5 select_maximum_fusion
  880.9 78.5 %fusion.31 = f32[24,152,200]{2,1,0:T(8,128)} fusion(f32[24,152,200]{2,1,0:T(8,128)} %get-tuple-element.77, f32[3,152,200]{2,1,0:T(8,128)S(1)} %get-tuple-element.84, f32[3,152,200]{2,1,0:T(8,128)S(1)} %get-tuple-element.83, f32[30,158,200]{2,1,0:T(8,128)} %select_maximum_fusion, bf16[24,152,200]{2,1,0:T(8,128)(2,1)S(1)} %copy-done.5, f32[200]{0:T(256)} %bitcast.48, ...), kind=kLoop, calls=%fused_computation.64 | loop fusion | flops 78796800 | bytes 130652992 | tf_op jit(solution)/shard_map/mul | solution.py:161
  959.4 3.7 copy.37
  963.1 1.6 copy.38
  (232 shorter events, 0.9 us)
Async XLA Ops:
  7.2 213.8 %copy-start = (bf16[800,800]{1,0:T(8,128)(2,1)S(1)}, bf16[800,800]{1,0:T(8,128)(2,1)}, u32[]{:S(2)}) copy-start(bf16[800,800]{1,0:T(8,128)(2,1)} %param.19) | copy-start | bytes 3840004
  7.2 213.8 %all-gather.3.cloned.1.call-start = ((), (), s32[]{:S(2)}) async-start(), calls=%async_computation.2 | async-start | bytes 7424000 | tf_op jit(solution)/shard_map/all_gather | solution.py:97
  8.1 7.1 copy-start.11
  10.1 5.6 copy-start.13
  15.2 2.1 collective-permute-start
  15.7 6.2 copy-start.22
  15.7 6.1 copy-start.24
  15.7 6.1 copy-start.26
  15.8 6.1 copy-start.28
  15.8 6.1 copy-start.30
  15.8 6.1 copy-start.32
  15.8 6.1 copy-start.34
  15.8 6.1 copy-start.36
  15.8 6.1 copy-start.38
  15.8 6.1 copy-start.40
  15.8 6.1 copy-start.42
  15.8 6.1 copy-start.44
  15.8 6.1 copy-start.46
  15.9 6.1 copy-start.48
  15.9 6.1 copy-start.50
  15.9 6.1 copy-start.52
  15.9 6.1 copy-start.54
  15.9 6.1 copy-start.56
  15.9 6.1 copy-start.58
  16.5 5.6 copy-start.62
  16.5 5.6 copy-start.64
  16.5 5.6 copy-start.66
  16.5 5.6 copy-start.68
  16.5 5.6 copy-start.70
  16.5 5.6 copy-start.72
  16.5 5.6 copy-start.74
  16.5 5.6 copy-start.76
  16.5 5.6 copy-start.78
  16.5 5.6 copy-start.80
  16.5 5.6 copy-start.82
  16.5 5.6 copy-start.84
  16.6 5.6 copy-start.86
  16.6 5.6 copy-start.88
  16.6 5.6 copy-start.90
  16.6 5.6 copy-start.92
  16.6 5.6 copy-start.94
  98.0 5.7 copy-start.16
  98.0 5.7 copy-start.97
  98.2 1.2 collective-permute-start.1
  99.5 6.8 copy-start.14
  102.3 1.2 collective-permute-start.2
  108.8 112.2 %copy-start.101 = (f32[800]{0:T(1024)S(1)}, f32[800]{0:T(1024)}, u32[]{:S(2)}) copy-start(f32[800]{0:T(1024)} %param.20) | copy-start | bytes 9604
  108.8 222.2 %all-gather.5.cloned.1.call-start = ((), (), s32[]{:S(2)}) async-start(), calls=%async_computation.3 | async-start | bytes 7424000 | tf_op jit(solution)/shard_map/all_gather | solution.py:103
  112.7 442.1 %reduce-scatter.9.cloned.1.call-start = ((), (), s32[]{:S(2)}) async-start(), calls=%async_computation.5 | async-start | bytes 14848000
  354.9 404.1 %reduce-scatter.7.cloned.1.call-start = ((), (), s32[]{:S(2)}) async-start(), calls=%async_computation.4 | async-start | bytes 14848000
  367.8 591.6 %all-reduce.8.cloned.1.call-start = ((), (), s32[]{:S(2)}) async-start(), calls=%async_computation.6 | async-start | bytes 11468800 | tf_op jit(solution)/shard_map/psum | solution.py:171
  390.7 164.1 %copy-start.17 = (f32[200]{0:T(256)S(1)}, f32[200]{0:T(256)}, u32[]{:S(2)}) copy-start(f32[200]{0:T(256)} %param.17) | copy-start | bytes 2404
  567.5 196.4 %copy-start.98 = (f32[200]{0:T(256)S(1)}, f32[200]{0:T(256)}, u32[]{:S(2)}) copy-start(f32[200]{0:T(256)} %param.22) | copy-start | bytes 2404
  567.7 200.3 %collective-permute-start.3 = (f32[2,2]{1,0:T(2,128)S(1)}, f32[2,2]{1,0:T(2,128)S(1)}, u32[]{:S(2)}, u32[]{:S(2)}) collective-permute-start(f32[2,2]{1,0:T(2,128)S(1)} %pad_maximum_fusion.4), channel_id=1, source_target_pairs={{0,4},{4,0},{8,12},{12,8},{16,20},{20,16},{24,28},{28,24},{1,5},{5... | collective-permute-start | bytes 56 | tf_op jit(solution)/shard_map/ppermute | solution.py:20
  768.4 77.2 %slice-start = ((s8[4915200]{0:T(1024)(128)(4,1)}), s8[720896]{0:T(1024)(128)(4,1)S(1)}, s32[]{:S(2)}) async-start(s8[4915200]{0:T(1024)(128)(4,1)} %bitcast.121), calls=%async_computation.7 | async-start | bytes 1441792
  806.5 30.1 %copy-start.2 = (f32[24,152,200]{2,1,0:T(8,128)S(1)}, f32[24,152,200]{2,1,0:T(8,128)}, u32[]{:S(2)}) copy-start(f32[24,152,200]{2,1,0:T(8,128)} %get-tuple-element.77) | copy-start | bytes 8755204
  806.5 30.2 %copy-start.3 = (f32[24,152,200]{2,1,0:T(8,128)S(1)}, f32[24,152,200]{2,1,0:T(8,128)}, u32[]{:S(2)}) copy-start(f32[24,152,200]{2,1,0:T(8,128)} %get-tuple-element.137) | copy-start | bytes 8755204
  806.5 30.2 %copy-start.4 = (bf16[24,152,200]{2,1,0:T(8,128)(2,1)S(1)}, bf16[24,152,200]{2,1,0:T(8,128)(2,1)}, u32[]{:S(2)}) copy-start(bf16[24,152,200]{2,1,0:T(8,128)(2,1)} %param.12) | copy-start | bytes 4377604
  806.5 30.2 %copy-start.7 = (f32[3,152,200]{2,1,0:T(8,128)S(1)}, f32[3,152,200]{2,1,0:T(8,128)}, u32[]{:S(2)}) copy-start(f32[3,152,200]{2,1,0:T(8,128)} %copy-done.6) | copy-start | bytes 1094404
  806.5 30.2 %copy-start.9 = (f32[3,152,200]{2,1,0:T(8,128)S(1)}, f32[3,152,200]{2,1,0:T(8,128)}, u32[]{:S(2)}) copy-start(f32[3,152,200]{2,1,0:T(8,128)} %copy-done.8) | copy-start | bytes 1094404
  806.6 30.2 %copy-start.12 = (f32[24,152]{1,0:T(8,128)S(1)}, f32[24,152]{1,0:T(8,128)}, u32[]{:S(2)}) copy-start(f32[24,152]{1,0:T(8,128)} %copy-done.11) | copy-start | bytes 43780
  806.6 30.2 %copy-start.21 = (f32[200]{0:T(256)S(1)}, f32[200]{0:T(256)}, u32[]{:S(2)}) copy-start(f32[200]{0:T(256)} %copy-done.20) | copy-start | bytes 2404
  806.6 39.0 %slice-start.1 = ((s8[4915200]{0:T(1024)(128)(4,1)}), s8[4194304]{0:T(1024)(128)(4,1)S(1)}, s32[]{:S(2)}) async-start(s8[4915200]{0:T(1024)(128)(4,1)} %bitcast.121), calls=%async_computation.8 | async-start | bytes 8388608
  845.6 30.0 %collective-permute-start.4 = (bf16[3,152,200]{2,1,0:T(8,128)(2,1)S(1)}, bf16[3,152,200]{2,1,0:T(8,128)(2,1)S(1)}, u32[]{:S(2)}, u32[]{:S(2)}) collective-permute-start(bf16[3,152,200]{2,1,0:T(8,128)(2,1)S(1)} %fusion.83), channel_id=1, source_target_pairs={{0,4},{4,0},{8,12},{12,8},{16,20},{20,16},{24,28},{28,24},{1,5},{5... | collective-permute-start | bytes 547208 | tf_op jit(solution)/shard_map/ppermute | solution.py:20
  (51 other events, 241.4 us)
Sparse Core Ops, SparseCore 0:
  109.0 111.9 all-gather.2
  223.1 107.8 all-gather.4
  355.0 199.7 reduce-scatter.8
  557.0 201.9 reduce-scatter.6
  763.4 99.3 all-reduce.7
where the time goes:
time: 979 us; the launch traced here: 971 us
  waiting for transfers between devices  540 us (55%)
  other arithmetic  269 us (27%)
  matrix products  91.5 us (9%)
  local copies, waits for them, and re-layouts  27.8 us (3%)
  blocking collectives  26.3 us (3%)
  between operations  15.6 us (2%)
    unnamed x7, waiting for transfers between devices  355 us
    all_gather x1, waiting for transfers between devices, body(): gathered = lax.all_gather(normed, 'chan', axis=1, tiled=True)  108 us
    reduce_sum x4, other arithmetic, body(): jnp.sum(grad_conv * padded[row_shift:row_shift + height, col_shift:col_sh...  80.4 us
    reduce_sum x6, other arithmetic, local_groups(): jnp.sum(values.reshape(height, across, local_ch // group_size, group_size...  78.8 us
    mul x1, other arithmetic, body(): grad_inputs = wet_cells * history_keep * (grad_res + grad_masked)  78.5 us
    all_gather x1, waiting for transfers between devices, body(): grad_gathered = lax.all_gather(grad_branch, 'chan', axis=1, tiled=True)  74.2 us
    dot_general x1, matrix products, body(): jnp.dot(gathered, weight_in, preferred_element_type=jnp.float32) + bias_in  35.8 us
    psum x1, blocking collectives, body(): lax.psum((grad_kernel, grad_conv_bias, grad_gain, grad_norm_bias, grad_we...  26.3 us
  transfers between devices with their start and end apart: 10, of which 6 were waited for; matrix products, arithmetic and copies ran while one was open for 27% of the time, Pallas kernels for 0%

commit v1 on v0

--- a/solution.py
+++ b/solution.py
@@ -8,6 +8,27 @@
 HISTORY = 2
 SPAN = 2
 EPSILON = 1e-05
+
+
+def gather_around(array, axis, dim):
+    size, index, width = (lax.axis_size(axis), lax.axis_index(axis), array.shape[dim])
+    right = [(i, (i + 1) % size) for i in range(size)]
+    backward = [(i, (i - 1) % size) for i in range(size)]
+    result = jnp.zeros((*array.shape[:dim], size * width, *array.shape[dim + 1 :]), array.dtype)
+    result = lax.dynamic_update_slice_in_dim(result, array, index * width, axis=dim)
+    from_left = from_right = array
+    half = size // 2
+    for step in range(1, half + 1):
+        from_left = lax.ppermute(from_left, axis, right)
+        result = lax.dynamic_update_slice_in_dim(
+            result, from_left, (index - step) % size * width, axis=dim
+        )
+        if step < size - half:
+            from_right = lax.ppermute(from_right, axis, backward)
+            result = lax.dynamic_update_slice_in_dim(
+                result, from_right, (index + step) % size * width, axis=dim
+            )
+    return result
 
 
 def swapped(block, axis, distance):
@@ -94,7 +115,7 @@
     grad_res = cotangent.astype(jnp.float32) * wet_cells
     grad_branch = grad_res.reshape(pixels, local_ch).astype(jnp.bfloat16)
     grad_bias_out = jnp.sum(grad_branch.astype(jnp.float32), 0)
-    gathered = lax.all_gather(normed, "chan", axis=1, tiled=True)
+    gathered = gather_around(normed, "chan", 1)
     hidden = jnp.dot(gathered, weight_in, preferred_element_type=jnp.float32) + bias_in
     active = jax.nn.gelu(hidden, approximate=False).astype(jnp.bfloat16)
     partial_value = jnp.dot(active, weight_out, preferred_element_type=jnp.float32)

time: 979 us -> 914 us (0.934)
  waiting for transfers between devices: 540 us -> 455 us
    all_gather x1 -> x0, waiting for transfers between devices: 108 us -> none  [body(): gathered = lax.all_gather(normed, 'chan', axis=1, tiled=True)]
    ppermute x0 -> x3, waiting for transfers between devices: none -> 98.1 us  [the longest x2 75.9 us: gather_around(): from_left = lax.ppermute(from_left, axis, right)]
    all_gather x1, waiting for transfers between devices: 74.2 us -> 0.01 us  [body(): grad_gathered = lax.all_gather(grad_branch, 'chan', axis=1, tiled=True)]
    unnamed x7 -> x6, waiting for transfers between devices: 355 us -> 355 us
  transfers between devices with their start and end apart: 10 -> 12, of which waited for: 6 -> 7; matrix products, arithmetic and copies ran while one was open for 27% -> 36% of each run, Pallas kernels for 0% -> 0%
where the time goes in v1:
time: 914 us; the launch traced here: 907 us
  waiting for transfers between devices  455 us (50%)
  other arithmetic  270 us (30%)
  matrix products  95.4 us (10%)
  local copies, waits for them, and re-layouts  37.4 us (4%)
  blocking collectives  26.4 us (3%)
  between operations  15.8 us (2%)
    unnamed x6, waiting for transfers between devices  355 us
    reduce_sum x4, other arithmetic, body(): jnp.sum(grad_conv * padded[row_shift:row_shift + height, col_shift:col_sh...  80.2 us
    reduce_sum x6, other arithmetic, local_groups(): jnp.sum(values.reshape(height, across, local_ch // group_size, group_size...  78.8 us
    mul x1, other arithmetic, body(): grad_inputs = wet_cells * history_keep * (grad_res + grad_masked)  78.5 us
    ppermute x2, waiting for transfers between devices, gather_around(): from_left = lax.ppermute(from_left, axis, right)  75.9 us
    dot_general x1, matrix products, body(): jnp.dot(gathered, weight_in, preferred_element_type=jnp.float32) + bias_in  42.4 us
    psum x1, blocking collectives, body(): lax.psum((grad_kernel, grad_conv_bias, grad_gain, grad_norm_bias, grad_we...  26.4 us
    ppermute x1, waiting for transfers between devices, gather_around(): from_right = lax.ppermute(from_right, axis, backward)  22.2 us
  transfers between devices with their start and end apart: 12, of which 7 were waited for; matrix products, arithmetic and copies ran while one was open for 36% of the time, Pallas kernels for 0%

profile of v1, /device:TPU:0, one launch (start us, length us, event | category | flops | bytes accessed | tf_op | source)
XLA Modules:
  0.0 906.6 jit_solution(15635170377378346630)
XLA Ops:
  7.3 0.8 convert_element_type.63
  8.1 1.3 fusion.84
  9.4 0.7 compare_convert_fusion
  10.1 5.1 convert_reduce_fusion.1
  15.1 2.5 copy.37
  17.7 1.1 slice_select_fusion.1
  18.8 0.5 collective-permute-start
  19.5 0.5 fusion.91
  20.2 0.6 fusion.92
  20.9 4.5 select_maximum_fusion.2
  25.8 75.7 %fusion.89 = (f32[200]{0:T(256)S(1)}, f32[24,152,200]{2,1,0:T(8,128)}) fusion(f32[200]{0:T(256)} %bitcast.48, f32[30,158,200]{2,1,0:T(8,128)} %select_maximum_fusion.2, f32[200]{0:T(256)} %bitcast.47, f32[200]{0:T(256)S(1)} %bitcast.130, f32[200]{0:T(256)S(1)} %bitcast.132, f32[3,152,200]{2,1,0:T(8,128)S(1)} %get-tuple-element.89, ...), kind=kLoop, calls=%fused_computation.246 | loop fusion | flops 76607800 | bytes 129180000 | tf_op jit(solution)/shard_map/reduce_sum | solution.py:50
  101.6 0.1 reduce_sum.561
  101.7 0.1 reduce_sum.562
  101.8 0.1 collective-permute-start.1
  101.9 1.1 collective-permute-done.1
  103.0 0.1 div.45
  103.1 2.6 multiply_reduce_fusion.51
  105.7 0.1 reduce_sum.564
  105.8 0.1 reduce_sum.565
  105.9 0.3 collective-permute-start.2
  106.2 0.9 collective-permute-done.2
  107.2 0.1 rsqrt.12
  107.3 2.7 add_convert_fusion
  109.9 2.5 copy.33
  112.4 2.8 collective-permute-start.3
  115.2 2.1 collective-permute-start.4
  117.3 44.5 %collective-permute-done.3 = bf16[3648,200]{0,1:T(8,128)(2,1)} collective-permute-done((bf16[3648,200]{0,1:T(8,128)(2,1)}, bf16[3648,200]{0,1:T(8,128)(2,1)}, u32[]{:S(2)}, u32[]{:S(2)}) %collective-permute-start.3) | collective-permute-done | bytes 1459232 | tf_op jit(solution)/shard_map/ppermute | solution.py:22
  161.8 0.2 collective-permute-start.5
  162.0 3.0 broadcast_in_dim.15
  165.0 1.2 constant_dynamic-update-slice_fusion.3
  166.2 2.7 constant_dynamic-update-slice_fusion.2
  169.0 22.2 %collective-permute-done.4 = bf16[3648,200]{0,1:T(8,128)(2,1)} collective-permute-done((bf16[3648,200]{0,1:T(8,128)(2,1)}, bf16[3648,200]{0,1:T(8,128)(2,1)}, u32[]{:S(2)}, u32[]{:S(2)}) %collective-permute-start.4) | collective-permute-done | bytes 1459232 | tf_op jit(solution)/shard_map/ppermute | solution.py:27
  191.1 2.6 constant_dynamic-update-slice_fusion.1
  193.8 31.4 %collective-permute-done.5 = bf16[3648,200]{0,1:T(8,128)(2,1)S(1)} collective-permute-done((bf16[3648,200]{0,1:T(8,128)(2,1)}, bf16[3648,200]{0,1:T(8,128)(2,1)S(1)}, u32[]{:S(2)}, u32[]{:S(2)}) %collective-permute-start.5) | collective-permute-done | bytes 1459232 | tf_op jit(solution)/shard_map/ppermute | solution.py:22
  225.2 1.2 constant_dynamic-update-slice_fusion
  226.4 9.2 %fusion.96 = f32[3648,800]{0,1:T(8,128)S(1)} fusion(bf16[800,800]{1,0:T(8,128)(2,1)S(1)} %copy-done.101, bf16[3648,800]{0,1:T(8,128)(2,1)} %all-gather.2.cloned.1.call-done), kind=kOutput, calls=%fused_computation.253 | convolution fusion | flops 4669440000 | bytes 18790400 | tf_op jit(solution)/shard_map/dot_general | solution.py:125
  235.6 42.4 %convert_reduce_fusion = (f32[800]{0:T(1024)S(1)}, bf16[3648,800]{0,1:T(8,128)(2,1)S(1)}, bf16[3648,800]{0,1:T(8,128)(2,1)}) fusion(f32[3648,800]{0,1:T(8,128)S(1)} %fusion.96, f32[800]{0:T(1024)S(1)} %copy-done.103, bf16[3648,800]{0,1:T(8,128)(2,1)} %constant_dynamic-update-slice_fusion, bf16[800,800]{1,0:T(8,128)(2,1)S(1)} %copy-done), kind=kOutput, calls=%fused_computation.11 | convolution fusion | flops 4897074176 | bytes 30470400 | tf_op jit(solution)/shard_map/dot_general | solution.py:119
  278.0 2.5 copy-done.104
  280.5 9.3 %fusion.97 = f32[3648,800]{0,1:T(8,128)} fusion(bf16[800,800]{1,0:T(8,128)(2,1)S(1)} %copy-done, bf16[3648,800]{0,1:T(8,128)(2,1)S(1)} %get-tuple-element.78), kind=kOutput, calls=%fused_computation.254 | convolution fusion | flops 4669440000 | bytes 18790400 | tf_op jit(solution)/shard_map/dot_general | solution.py:136
  289.8 1.3 copy-done.102
  291.1 11.6 %fusion.93 = f32[3648,800]{0,1:T(8,128)} fusion(bf16[3648,800]{0,1:T(8,128)(2,1)} %get-tuple-element.82, bf16[800,800]{1,0:T(8,128)(2,1)S(1)} %copy-done.102), kind=kOutput, calls=%fused_computation.250 | convolution fusion | flops 4669440000 | bytes 18790400 | tf_op jit(solution)/shard_map/dot_general | solution.py:121
  302.8 11.4 %fusion.94 = f32[800,800]{1,0:T(8,128)} fusion(bf16[3648,800]{0,1:T(8,128)(2,1)} %constant_dynamic-update-slice_fusion, bf16[3648,800]{0,1:T(8,128)(2,1)} %copy-done.104), kind=kOutput, calls=%fused_computation.251 | convolution fusion | flops 4669440000 | bytes 14233600 | tf_op jit(solution)/shard_map/dot_general | solution.py:133
  314.2 11.4 %fusion.95 = f32[800,800]{1,0:T(8,128)} fusion(bf16[3648,800]{0,1:T(8,128)(2,1)} %get-tuple-element.82, bf16[3648,800]{0,1:T(8,128)(2,1)} %all-gather.2.cloned.1.call-done), kind=kOutput, calls=%fused_computation.252 | convolution fusion | flops 4669440000 | bytes 14233600 | tf_op jit(solution)/shard_map/dot_general | solution.py:128
  325.7 163.8 %reduce-scatter.9.cloned.1.call-done = f32[3648,200]{0,1:T(8,128)} async-done(((f32[3648,800]{0,1:T(8,128)}), f32[3648,200]{0,1:T(8,128)}) %reduce-scatter.9.cloned.1.call-update) | async-done | bytes 2918416
  489.6 2.3 fusion.86
  491.9 0.1 reduce_sum.568
  492.0 4.9 copy.38
  496.9 5.3 multiply_reduce_fusion
  502.3 0.1 reduce_sum.571
  502.5 191.4 %reduce-scatter.7.cloned.1.call-done = f32[3648,200]{0,1:T(8,128)} async-done(((f32[3648,800]{0,1:T(8,128)}), f32[3648,200]{0,1:T(8,128)}) %reduce-scatter.7.cloned.1.call-update) | async-done | bytes 2918416
  693.9 4.9 copy.36
  698.8 4.1 broadcast_add_fusion
  703.0 0.1 div.49
  703.2 0.1 div.52
  703.3 37.9 %multiply_reduce_fusion.1 = (f32[200]{0:T(256)S(1)}, f32[200]{0:T(256)S(1)}, f32[200]{0:T(256)S(1)}, f32[200]{0:T(256)S(1)}, f32[200]{0:T(256)S(1)}, /*index=5*/...) fusion(f32[30,158,200]{2,1,0:T(8,128)} %select_maximum_fusion.2, ...), kind=kLoop, calls=%fused_computation.162 | loop fusion | flops 31369200 | bytes 61304800 | tf_op jit(solution)/shard_map/reduce_sum | solution.py:160
  741.3 30.1 %multiply_reduce_fusion.2 = (f32[200]{0:T(256)S(1)}, f32[200]{0:T(256)S(1)}, f32[200]{0:T(256)S(1)}, f32[200]{0:T(256)S(1)}, f32[200]{0:T(256)S(1)}, /*index=5*/...) fusion(f32[24,152,200]{2,1,0:T(8,128)} %get-tuple-element.79, ...), kind=kLoop, calls=%fused_computation.163 | loop fusion | flops 26262000 | bytes 55464000 | tf_op jit(solution)/shard_map/reduce_sum | solution.py:160
  771.6 8.8 multiply_reduce_fusion.4
  780.4 3.4 multiply_reduce_fusion.43
  783.8 0.2 stack.211
  784.0 26.4 %all-reduce.4 = (f32[7,7,200]{2,1,0:T(8,128)}, f32[200]{0:T(256)}, f32[200]{0:T(256)}, f32[200]{0:T(256)}, f32[800]{0:T(1024)}, /*index=5*/f32[200]{0:T(256)}) all-reduce(f32[7,7,200]{2,1,0:T(8,128)S(1)} %reshape.110, f32[200]{0:T(256)S(1)} %get-tuple-element.63, ...), channel_id=1, replica_groups=mesh['dp'=8,'chan'=4] {'dp'}, use_global_device_ids=true, to_apply=%region_60.61 | all-reduce | flops 11400 | bytes 91200 | tf_op jit(solution)/shard_map/psum | solution.py:192
  810.9 4.5 select_maximum_fusion
  815.7 78.5 %fusion.31 = f32[24,152,200]{2,1,0:T(8,128)} fusion(f32[24,152,200]{2,1,0:T(8,128)} %get-tuple-element.79, f32[3,152,200]{2,1,0:T(8,128)S(1)} %get-tuple-element.87, f32[3,152,200]{2,1,0:T(8,128)S(1)} %get-tuple-element.86, f32[30,158,200]{2,1,0:T(8,128)} %select_maximum_fusion, bf16[24,152,200]{2,1,0:T(8,128)(2,1)S(1)} %copy-done.5, f32[200]{0:T(256)} %bitcast.48, ...), kind=kLoop, calls=%fused_computation.64 | loop fusion | flops 78796800 | bytes 130652992 | tf_op jit(solution)/shard_map/mul | solution.py:182
  894.3 3.7 copy.45
  898.0 1.6 copy.46
  (244 shorter events, 1.5 us)
Async XLA Ops:
  7.2 228.4 %copy-start = (bf16[800,800]{1,0:T(8,128)(2,1)S(1)}, bf16[800,800]{1,0:T(8,128)(2,1)}, u32[]{:S(2)}) copy-start(bf16[800,800]{1,0:T(8,128)(2,1)} %param.19) | copy-start | bytes 3840004
  7.2 219.2 %all-gather.2.cloned.1.call-start = ((), (), s32[]{:S(2)}) async-start(), calls=%async_computation.2 | async-start | bytes 7424000 | tf_op jit(solution)/shard_map/all_gather | solution.py:124
  8.1 7.0 copy-start.12
  17.6 471.9 %reduce-scatter.9.cloned.1.call-start = ((), (), s32[]{:S(2)}) async-start(), calls=%async_computation.4 | async-start | bytes 14848000
  18.8 2.1 collective-permute-start
  19.3 6.2 copy-start.23
  19.3 6.1 copy-start.25
  19.3 6.1 copy-start.27
  19.3 6.1 copy-start.29
  19.3 6.1 copy-start.31
  19.3 6.1 copy-start.33
  19.4 6.1 copy-start.35
  19.4 6.1 copy-start.37
  19.4 6.1 copy-start.39
  19.4 6.1 copy-start.41
  19.4 6.1 copy-start.43
  19.4 6.1 copy-start.45
  19.4 6.1 copy-start.47
  19.4 6.1 copy-start.49
  19.4 6.1 copy-start.51
  19.4 6.1 copy-start.53
  19.5 6.1 copy-start.55
  19.5 6.1 copy-start.57
  19.5 6.1 copy-start.59
  20.0 5.6 copy-start.69
  20.1 5.6 copy-start.71
  20.1 5.6 copy-start.73
  20.1 5.6 copy-start.75
  20.1 5.6 copy-start.77
  20.1 5.6 copy-start.79
  20.1 5.6 copy-start.81
  20.1 5.6 copy-start.83
  20.1 5.6 copy-start.85
  20.1 5.6 copy-start.87
  20.1 5.6 copy-start.89
  20.1 5.6 copy-start.91
  20.2 5.6 copy-start.93
  20.2 5.6 copy-start.95
  101.5 5.7 copy-start.17
  101.6 5.7 copy-start.98
  101.8 1.2 collective-permute-start.1
  103.1 6.8 copy-start.15
  105.9 1.2 collective-permute-start.2
  112.4 52.6 %copy-start.10 = (bf16[3648,200]{0,1:T(8,128)(2,1)S(1)}, bf16[3648,200]{0,1:T(8,128)(2,1)}, u32[]{:S(2)}) copy-start(bf16[3648,200]{0,1:T(8,128)(2,1)} %copy.33) | copy-start | bytes 4377604
  112.4 49.4 %collective-permute-start.3 = (bf16[3648,200]{0,1:T(8,128)(2,1)}, bf16[3648,200]{0,1:T(8,128)(2,1)}, u32[]{:S(2)}, u32[]{:S(2)}) collective-permute-start(bf16[3648,200]{0,1:T(8,128)(2,1)} %copy.33), channel_id=1, source_target_pairs={{0,1},{1,2},{2,3},{3,0},{4,5},{5,6},{6,7},{7,4},{8,9},{9,10},{10,1... | collective-permute-start | bytes 4377608 | tf_op jit(solution)/shard_map/ppermute | solution.py:22
  115.2 76.0 %collective-permute-start.4 = (bf16[3648,200]{0,1:T(8,128)(2,1)}, bf16[3648,200]{0,1:T(8,128)(2,1)}, u32[]{:S(2)}, u32[]{:S(2)}) collective-permute-start(bf16[3648,200]{0,1:T(8,128)(2,1)} %copy.33), channel_id=1, source_target_pairs={{0,3},{1,0},{2,1},{3,2},{4,7},{5,4},{6,5},{7,6},{8,11},{9,8},{10,9... | collective-permute-start | bytes 4377608 | tf_op jit(solution)/shard_map/ppermute | solution.py:27
  161.8 63.4 %collective-permute-start.5 = (bf16[3648,200]{0,1:T(8,128)(2,1)}, bf16[3648,200]{0,1:T(8,128)(2,1)S(1)}, u32[]{:S(2)}, u32[]{:S(2)}) collective-permute-start(bf16[3648,200]{0,1:T(8,128)(2,1)} %collective-permute-done.3), channel_id=1, source_target_pairs={{0,1},{1,2},{2,3},{3,0},{4,5},{5,6},{6,7},{7,4},{8,9},{9,10},{10,1... | collective-permute-start | bytes 4377608 | tf_op jit(solution)/shard_map/ppermute | solution.py:22
  166.2 60.2 %copy-start.101 = (bf16[800,800]{1,0:T(8,128)(2,1)S(1)}, bf16[800,800]{1,0:T(8,128)(2,1)}, u32[]{:S(2)}) copy-start(bf16[800,800]{1,0:T(8,128)(2,1)} %param.21) | copy-start | bytes 3840004
  226.4 9.2 %copy-start.103 = (f32[800]{0:T(1024)S(1)}, f32[800]{0:T(1024)}, u32[]{:S(2)}) copy-start(f32[800]{0:T(1024)} %param.20) | copy-start | bytes 9604
  289.8 404.1 %reduce-scatter.7.cloned.1.call-start = ((), (), s32[]{:S(2)}) async-start(), calls=%async_computation.3 | async-start | bytes 14848000
  302.8 591.5 %all-reduce.8.cloned.1.call-start = ((), (), s32[]{:S(2)}) async-start(), calls=%async_computation.5 | async-start | bytes 11468800 | tf_op jit(solution)/shard_map/psum | solution.py:192
  325.7 163.9 %copy-start.18 = (f32[200]{0:T(256)S(1)}, f32[200]{0:T(256)}, u32[]{:S(2)}) copy-start(f32[200]{0:T(256)} %param.17) | copy-start | bytes 2404
  502.2 196.6 %copy-start.99 = (f32[200]{0:T(256)S(1)}, f32[200]{0:T(256)}, u32[]{:S(2)}) copy-start(f32[200]{0:T(256)} %param.22) | copy-start | bytes 2404
  502.4 200.5 %collective-permute-start.6 = (f32[2,2]{1,0:T(2,128)S(1)}, f32[2,2]{1,0:T(2,128)S(1)}, u32[]{:S(2)}, u32[]{:S(2)}) collective-permute-start(f32[2,2]{1,0:T(2,128)S(1)} %pad_maximum_fusion.4), channel_id=1, source_target_pairs={{0,4},{4,0},{8,12},{12,8},{16,20},{20,16},{24,28},{28,24},{1,5},{5... | collective-permute-start | bytes 56 | tf_op jit(solution)/shard_map/ppermute | solution.py:41
  703.3 77.1 %slice-start = ((s8[4915200]{0:T(1024)(128)(4,1)}), s8[720896]{0:T(1024)(128)(4,1)S(1)}, s32[]{:S(2)}) async-start(s8[4915200]{0:T(1024)(128)(4,1)} %bitcast.121), calls=%async_computation.6 | async-start | bytes 1441792
  741.2 30.1 %copy-start.2 = (f32[24,152,200]{2,1,0:T(8,128)S(1)}, f32[24,152,200]{2,1,0:T(8,128)}, u32[]{:S(2)}) copy-start(f32[24,152,200]{2,1,0:T(8,128)} %get-tuple-element.79) | copy-start | bytes 8755204
  741.2 30.3 %copy-start.3 = (f32[24,152,200]{2,1,0:T(8,128)S(1)}, f32[24,152,200]{2,1,0:T(8,128)}, u32[]{:S(2)}) copy-start(f32[24,152,200]{2,1,0:T(8,128)} %get-tuple-element.140) | copy-start | bytes 8755204
  741.2 30.3 %copy-start.4 = (bf16[24,152,200]{2,1,0:T(8,128)(2,1)S(1)}, bf16[24,152,200]{2,1,0:T(8,128)(2,1)}, u32[]{:S(2)}) copy-start(bf16[24,152,200]{2,1,0:T(8,128)(2,1)} %param.12) | copy-start | bytes 4377604
  741.2 30.3 %copy-start.7 = (f32[3,152,200]{2,1,0:T(8,128)S(1)}, f32[3,152,200]{2,1,0:T(8,128)}, u32[]{:S(2)}) copy-start(f32[3,152,200]{2,1,0:T(8,128)} %copy-done.6) | copy-start | bytes 1094404
  741.3 30.3 %copy-start.9 = (f32[3,152,200]{2,1,0:T(8,128)S(1)}, f32[3,152,200]{2,1,0:T(8,128)}, u32[]{:S(2)}) copy-start(f32[3,152,200]{2,1,0:T(8,128)} %copy-done.8) | copy-start | bytes 1094404
  741.3 30.3 %copy-start.13 = (f32[24,152]{1,0:T(8,128)S(1)}, f32[24,152]{1,0:T(8,128)}, u32[]{:S(2)}) copy-start(f32[24,152]{1,0:T(8,128)} %copy-done.12) | copy-start | bytes 43780
  741.3 30.3 %copy-start.22 = (f32[200]{0:T(256)S(1)}, f32[200]{0:T(256)}, u32[]{:S(2)}) copy-start(f32[200]{0:T(256)} %copy-done.21) | copy-start | bytes 2404
  741.3 39.1 %slice-start.1 = ((s8[4915200]{0:T(1024)(128)(4,1)}), s8[4194304]{0:T(1024)(128)(4,1)S(1)}, s32[]{:S(2)}) async-start(s8[4915200]{0:T(1024)(128)(4,1)} %bitcast.121), calls=%async_computation.7 | async-start | bytes 8388608
  771.4 39.0 %collective-permute-start.7 = (bf16[3,152,200]{2,1,0:T(8,128)(2,1)S(1)}, bf16[3,152,200]{2,1,0:T(8,128)(2,1)S(1)}, u32[]{:S(2)}, u32[]{:S(2)}) collective-permute-start(bf16[3,152,200]{2,1,0:T(8,128)(2,1)S(1)} %fusion.83), channel_id=1, source_target_pairs={{0,4},{4,0},{8,12},{12,8},{16,20},{20,16},{24,28},{28,24},{1,5},{5... | collective-permute-start | bytes 547208 | tf_op jit(solution)/shard_map/ppermute | solution.py:41
  (55 other events, 262.2 us)
Sparse Core Ops, SparseCore 0:
  17.7 150.7 all-gather.1
  289.9 199.5 reduce-scatter.8
  491.9 201.9 reduce-scatter.6
  698.3 99.3 all-reduce.7
